TPU v7x, 32 devices: a whole 2x2x4 slice. The times are simulated.
32 devices in a mesh: win: 2 (over x), sub: 16 (over z, y, core).
Axes of the slice: x: 2, y: 2, z: 4, core: 2. Of those that a mesh axis runs over, the one named last changes fastest.
Arguments:
- pulses: bfloat16 [32, 80, 2, 4096], P(('win', 'sub')), parts along dimension 0, may hold values from -6 to 6
- offsets: int32 [32, 80], P(('win', 'sub')), parts along dimension 0, may hold values from 0 to 3968
- geometry: float32 [32, 3, 80], P(('win', 'sub')), parts along dimension 0, may hold values from -1 to 1
- counts: int32 [32], P(('win', 'sub')), parts along dimension 0, may hold values from 48 to 80, as said below
Outputs:
- frames: float32 [32, 2, 32, 512], P(('win', 'sub')), parts along dimension 0
- cumulative: float32 [32, 2, 32, 512], P(('win', 'sub')), parts along dimension 0
There are 2 independent parts, one for each index of `win`. A program takes and returns all parts, laid end to end along the dimension named above; each array names one. Nothing has to cross between parts.
Inputs may be any that keep to these rules, and one draw needn't show every extreme that they name: Subaperture s holds its pulses in slots 0 to counts[s] - 1; the other slots are unused. Some subaperture has 80 pulses and some 48.
All inputs are finite; a program needn't handle non-finite values.
Results may differ from a plain program's by a relative error of at most 0.004.
Values sent between devices are 32-bit elements; how exact they have to be, the bound alone decides.
A program may use at most 192 MiB of HBM per device.

v0:
```python
import math
import jax
import jax.numpy as jnp
from jax import lax
from jax.sharding import PartitionSpec as P

ROWS = 32
COLS = 512
BINS = 128


def spectrum_of(pulse_rows, vertical_offset_along, geometry_sub, count, width):
    slots = pulse_rows.shape[0]
    windows = jax.vmap(lambda one_row, offset: lax.dynamic_slice_in_dim(one_row, offset, width, 1))(
        pulse_rows, vertical_offset_along
    ).astype(jnp.float32)
    index = jnp.arange(width, dtype=jnp.int32)
    shifted = index - width // 2
    turns = index[:, None] * shifted[None, :] % width
    angle = 2.0 * math.pi / width * turns.astype(jnp.float32)
    cosine = jnp.cos(angle)
    sine = jnp.sin(angle)
    highest = lax.Precision.HIGHEST
    real_in = windows[:, 0]
    imag_in = windows[:, 1]
    real_out = (
        jnp.dot(real_in, cosine, precision=highest) + jnp.dot(imag_in, sine, precision=highest)
    ) / width
    imag_out = (
        jnp.dot(imag_in, cosine, precision=highest) - jnp.dot(real_in, sine, precision=highest)
    ) / width
    viewing_bearing = 2.0 * math.pi * (shifted.astype(jnp.float32) / width + 0.37)
    scene_middle = width / 2.0 + width / 16.0 * geometry_sub[0]
    radar_frequency = 2.0 * math.pi / 100.0 * (37 * vertical_offset_along % 100).astype(jnp.float32)
    signal_argument = viewing_bearing[None, :] * scene_middle[:, None] + radar_frequency[:, None]
    live = (jnp.arange(slots, dtype=jnp.int32) < count).astype(jnp.float32) / math.sqrt(slots)
    cos_phase = jnp.cos(signal_argument)
    sin_phase = jnp.sin(signal_argument)
    coefficient_real = live[:, None] * (real_out * cos_phase - imag_out * sin_phase)
    coef_im = live[:, None] * (real_out * sin_phase + imag_out * cos_phase)
    return (coefficient_real, coef_im, viewing_bearing)


def block_product(
    coefficient_real, coef_im, viewing_bearing, row_slope, column_gradient, rows, cols
):
    xpos = (jnp.arange(rows, dtype=jnp.int32) - rows // 2).astype(jnp.float32)
    ypos = (jnp.arange(cols, dtype=jnp.int32) - cols // 2).astype(jnp.float32)
    angle_x = xpos[:, None, None] * (viewing_bearing[None, :] * row_slope[:, None])[None]
    cosine_x = jnp.cos(angle_x)
    sine_x = jnp.sin(angle_x)
    left_re = coefficient_real[None] * cosine_x - coef_im[None] * sine_x
    left_im = coefficient_real[None] * sine_x + coef_im[None] * cosine_x
    left = jnp.concatenate([left_re.reshape(rows, -1), left_im.reshape(rows, -1)], axis=1).astype(
        jnp.bfloat16
    )
    angle_y = (viewing_bearing[None, :] * column_gradient[:, None])[:, :, None] * ypos[
        None, None, :
    ]
    right_re = jnp.cos(angle_y).reshape(-1, cols)
    right_im = jnp.sin(angle_y).reshape(-1, cols)
    upper = jnp.concatenate([right_re, right_im], axis=1)
    lower = jnp.concatenate([-right_im, right_re], axis=1)
    right = jnp.concatenate([upper, lower], axis=0).astype(jnp.bfloat16)
    return jnp.dot(left, right, preferred_element_type=jnp.float32)


def shards(pulses, offsets, geometry, counts):
    rows = ROWS
    cols = COLS
    width = BINS
    slots = pulses.shape[1]
    count = counts[0]
    geometry_sub = geometry[0]
    coefficient_real, coef_im, viewing_bearing = spectrum_of(
        pulses[0], offsets[0], geometry_sub, count, width
    )
    row_slope = 0.05 * geometry_sub[1]
    column_gradient = 0.05 * geometry_sub[2]

    def add_block(step, total):
        start = (step * 8).astype(jnp.int32)
        part_re = lax.dynamic_slice_in_dim(coefficient_real, start, 8, 0)
        part_im = lax.dynamic_slice_in_dim(coef_im, start, 8, 0)
        slope_r = lax.dynamic_slice_in_dim(row_slope, start, 8, 0)
        slope_c = lax.dynamic_slice_in_dim(column_gradient, start, 8, 0)
        return total + block_product(
            part_re, part_im, viewing_bearing, slope_r, slope_c, rows, cols
        )

    empty = jnp.zeros((rows, 2 * cols), jnp.float32)
    total = lax.fori_loop(0, slots // 8, add_block, empty)
    own = jnp.stack([total[:, :cols], total[:, cols:]], axis=0)[None]
    flattened = own.reshape(1, 2 * rows * cols)
    by_pixels = lax.all_to_all(flattened, "sub", split_axis=1, concat_axis=0, tiled=True)
    members = by_pixels.shape[0]
    running = jnp.cumsum(by_pixels, axis=0)
    delayed = jnp.concatenate([jnp.zeros((8, running.shape[1]), jnp.float32), running[:-8]], axis=0)
    frame_rows = (running - delayed) / math.sqrt(8.0)
    magnitude_factor = jnp.sqrt(jnp.arange(1, members + 1, dtype=jnp.int32).astype(jnp.float32))
    cumulative_rows = running / magnitude_factor[:, None]
    frames_back, cumulative_back = (
        lax.all_to_all(frame_rows, "sub", split_axis=0, concat_axis=1, tiled=True),
        lax.all_to_all(cumulative_rows, "sub", split_axis=0, concat_axis=1, tiled=True),
    )
    frames = frames_back.reshape(1, 2, rows, cols)
    cumulative = cumulative_back.reshape(1, 2, rows, cols)
    return (frames, cumulative)


def solution(mesh):
    return jax.shard_map(
        shards,
        mesh=mesh,
        in_specs=(
            P(("win", "sub"), None, None, None),
            P(("win", "sub"), None),
            P(("win", "sub"), None, None),
            P(("win", "sub")),
        ),
        out_specs=(P(("win", "sub"), None, None, None), P(("win", "sub"), None, None, None)),
        check_vma=False,
    )
```

profile of v0, /device:TPU:0, one launch (start us, length us, event | category | flops | bytes accessed | tf_op | source)
XLA Modules:
  0.0 226.5 jit_solution(11494692594200224226)
XLA Ops:
  0.7 56.8 %copy.10 = bf16[1,80,2,4096]{2,1,3,0:T(8,128)(2,1)} copy(bf16[1,80,2,4096]{3,2,1,0:T(2,128)(2,1)} %param.6) | data formatting | bytes 2621440 | tf_op args[0]
  57.5 17.8 %gather_fusion = bf16[80,2,128]{1,0,2:T(8,128)(2,1)S(1)} fusion(bf16[80,2,4096]{1,0,2:T(8,128)(2,1)} %bitcast.1, s32[80]{0:T(128)S(1)} %fusion.56), kind=kCustom, calls=%fused_computation | custom fusion | bytes 82880 | tf_op jit(solution)/shard_map/vmap()/gather | solution.py:14
  75.3 3.2 %fusion.73 = (bf16[80,1,128]{1,0,2:T(8,128)(2,1)}, bf16[80,1,128]{1,0,2:T(8,128)(2,1)}) fusion(bf16[80,2,128]{1,0,2:T(8,128)(2,1)S(1)} %gather_fusion), kind=kLoop, calls=%fused_computation.101 | loop fusion | bytes 81920 | tf_op jit(solution)/shard_map/slice | solution.py:24
  78.4 3.1 %copy.11 = bf16[80,1,128]{2,0,1:T(8,128)(2,1)S(1)} copy(bf16[80,1,128]{1,0,2:T(8,128)(2,1)} %get-tuple-element.243) | data formatting | bytes 40960 | tf_op jit(solution)/shard_map/slice | solution.py:24
  81.5 1.6 copy.12
  85.1 0.4 add_multiply_fusion.1
  85.5 100.0 %while.17 = (s32[]{:T(128)}, f32[32,1024]{1,0:T(8,128)S(1)}, f32[80,128]{1,0:T(8,128)S(1)}, f32[80]{0:T(128)S(1)}, f32[80,128]{1,0:T(8,128)S(1)}, /*index=5*/f32...) while((s32[]{:T(128)}, f32[32,1024]{1,0:T(8,128)S(1)}, ...), condition=%wide.region_1.2_spmd.clone.clone, body=%wide.region_0.1_spmd.clone.clone.sunk | while | flops 154242752 | bytes 6879337 | solution.py:92
  85.9 0.6 fusion.82
  86.7 8.2 %fusion.81 = (bf16[1024,512]{1,0:T(8,128)(2,1)S(1)}, bf16[1024,512]{1,0:T(8,128)(2,1)S(1)}, bf16[1024,512]{1,0:T(8,128)(2,1)S(1)}) fusion(f32[512]{0:T(512)S(1)} %add_convert_fusion.4, f32[1024]{0:T(1024)S(1)} %bitcast_multiply_fusion.4), kind=kLoop, calls=%fused_computation.13.clone.1 | loop fusion | flops 2621440 | bytes 3151872 | tf_op jit(solution)/shard_map/convert.5
  94.9 0.8 fusion.83
  95.9 0.6 fusion.82
  96.6 8.2 %fusion.81 = (bf16[1024,512]{1,0:T(8,128)(2,1)S(1)}, bf16[1024,512]{1,0:T(8,128)(2,1)S(1)}, bf16[1024,512]{1,0:T(8,128)(2,1)S(1)}) fusion(f32[512]{0:T(512)S(1)} %add_convert_fusion.4, f32[1024]{0:T(1024)S(1)} %bitcast_multiply_fusion.4), kind=kLoop, calls=%fused_computation.13.clone.1 | loop fusion | flops 2621440 | bytes 3151872 | tf_op jit(solution)/shard_map/convert.5
  104.9 0.8 fusion.83
  105.9 0.6 fusion.82
  106.6 8.2 %fusion.81 = (bf16[1024,512]{1,0:T(8,128)(2,1)S(1)}, bf16[1024,512]{1,0:T(8,128)(2,1)S(1)}, bf16[1024,512]{1,0:T(8,128)(2,1)S(1)}) fusion(f32[512]{0:T(512)S(1)} %add_convert_fusion.4, f32[1024]{0:T(1024)S(1)} %bitcast_multiply_fusion.4), kind=kLoop, calls=%fused_computation.13.clone.1 | loop fusion | flops 2621440 | bytes 3151872 | tf_op jit(solution)/shard_map/convert.5
  114.9 0.8 fusion.83
  115.9 0.6 fusion.82
  116.6 8.2 %fusion.81 = (bf16[1024,512]{1,0:T(8,128)(2,1)S(1)}, bf16[1024,512]{1,0:T(8,128)(2,1)S(1)}, bf16[1024,512]{1,0:T(8,128)(2,1)S(1)}) fusion(f32[512]{0:T(512)S(1)} %add_convert_fusion.4, f32[1024]{0:T(1024)S(1)} %bitcast_multiply_fusion.4), kind=kLoop, calls=%fused_computation.13.clone.1 | loop fusion | flops 2621440 | bytes 3151872 | tf_op jit(solution)/shard_map/convert.5
  124.8 0.8 fusion.83
  125.9 0.6 fusion.82
  126.6 8.2 %fusion.81 = (bf16[1024,512]{1,0:T(8,128)(2,1)S(1)}, bf16[1024,512]{1,0:T(8,128)(2,1)S(1)}, bf16[1024,512]{1,0:T(8,128)(2,1)S(1)}) fusion(f32[512]{0:T(512)S(1)} %add_convert_fusion.4, f32[1024]{0:T(1024)S(1)} %bitcast_multiply_fusion.4), kind=kLoop, calls=%fused_computation.13.clone.1 | loop fusion | flops 2621440 | bytes 3151872 | tf_op jit(solution)/shard_map/convert.5
  134.8 0.8 fusion.83
  135.8 0.6 fusion.82
  136.6 8.2 %fusion.81 = (bf16[1024,512]{1,0:T(8,128)(2,1)S(1)}, bf16[1024,512]{1,0:T(8,128)(2,1)S(1)}, bf16[1024,512]{1,0:T(8,128)(2,1)S(1)}) fusion(f32[512]{0:T(512)S(1)} %add_convert_fusion.4, f32[1024]{0:T(1024)S(1)} %bitcast_multiply_fusion.4), kind=kLoop, calls=%fused_computation.13.clone.1 | loop fusion | flops 2621440 | bytes 3151872 | tf_op jit(solution)/shard_map/convert.5
  144.8 0.8 fusion.83
  145.8 0.6 fusion.82
  146.5 8.2 %fusion.81 = (bf16[1024,512]{1,0:T(8,128)(2,1)S(1)}, bf16[1024,512]{1,0:T(8,128)(2,1)S(1)}, bf16[1024,512]{1,0:T(8,128)(2,1)S(1)}) fusion(f32[512]{0:T(512)S(1)} %add_convert_fusion.4, f32[1024]{0:T(1024)S(1)} %bitcast_multiply_fusion.4), kind=kLoop, calls=%fused_computation.13.clone.1 | loop fusion | flops 2621440 | bytes 3151872 | tf_op jit(solution)/shard_map/convert.5
  154.8 0.8 fusion.83
  155.8 0.6 fusion.82
  156.5 8.2 %fusion.81 = (bf16[1024,512]{1,0:T(8,128)(2,1)S(1)}, bf16[1024,512]{1,0:T(8,128)(2,1)S(1)}, bf16[1024,512]{1,0:T(8,128)(2,1)S(1)}) fusion(f32[512]{0:T(512)S(1)} %add_convert_fusion.4, f32[1024]{0:T(1024)S(1)} %bitcast_multiply_fusion.4), kind=kLoop, calls=%fused_computation.13.clone.1 | loop fusion | flops 2621440 | bytes 3151872 | tf_op jit(solution)/shard_map/convert.5
  164.8 0.8 fusion.83
  165.8 0.6 fusion.82
  166.5 8.2 %fusion.81 = (bf16[1024,512]{1,0:T(8,128)(2,1)S(1)}, bf16[1024,512]{1,0:T(8,128)(2,1)S(1)}, bf16[1024,512]{1,0:T(8,128)(2,1)S(1)}) fusion(f32[512]{0:T(512)S(1)} %add_convert_fusion.4, f32[1024]{0:T(1024)S(1)} %bitcast_multiply_fusion.4), kind=kLoop, calls=%fused_computation.13.clone.1 | loop fusion | flops 2621440 | bytes 3151872 | tf_op jit(solution)/shard_map/convert.5
  174.7 0.8 fusion.83
  175.8 0.6 fusion.82
  176.5 8.2 %fusion.81 = (bf16[1024,512]{1,0:T(8,128)(2,1)S(1)}, bf16[1024,512]{1,0:T(8,128)(2,1)S(1)}, bf16[1024,512]{1,0:T(8,128)(2,1)S(1)}) fusion(f32[512]{0:T(512)S(1)} %add_convert_fusion.4, f32[1024]{0:T(1024)S(1)} %bitcast_multiply_fusion.4), kind=kLoop, calls=%fused_computation.13.clone.1 | loop fusion | flops 2621440 | bytes 3151872 | tf_op jit(solution)/shard_map/convert.5
  184.7 0.8 fusion.83
  185.6 0.8 all_to_all.30
  186.4 7.4 %all-to-all-start = ((f32[1,16,2048]{2,0,1:T(1,128)}), f32[1,16,2048]{2,0,1:T(1,128)S(1)}, u32[]{:S(2)}, u32[]{:S(2)}) async-start(f32[1,16,2048]{2,0,1:T(1,128)} %all_to_all.30), calls=%async_computation | async-start | bytes 262144 | tf_op jit(solution)/shard_map/all_to_all | solution.py:95
  193.8 7.9 %all-to-all-done = f32[1,16,2048]{2,0,1:T(1,128)S(1)} async-done(((f32[1,16,2048]{2,0,1:T(1,128)}), f32[1,16,2048]{2,0,1:T(1,128)S(1)}, u32[]{:S(2)}, u32[]{:S(2)}) %all-to-all-start) | async-done | bytes 131104 | tf_op jit(solution)/shard_map/all_to_all | solution.py:95
  201.9 0.8 copy.13
  202.7 3.5 %all-to-all-start.1 = ((f32[16,1,2048]{2,1,0:T(1,128)}), f32[16,1,2048]{2,1,0:T(1,128)S(1)}, u32[]{:S(2)}, u32[]{:S(2)}) async-start(f32[16,1,2048]{2,1,0:T(1,128)} %copy.13), calls=%async_computation.1 | async-start | bytes 262144 | tf_op jit(solution)/shard_map/all_to_all | solution.py:103
  206.3 0.8 copy.14
  207.1 7.0 %all-to-all-done.1 = f32[16,1,2048]{2,1,0:T(1,128)S(1)} async-done(((f32[16,1,2048]{2,1,0:T(1,128)}), f32[16,1,2048]{2,1,0:T(1,128)S(1)}, u32[]{:S(2)}, u32[]{:S(2)}) %all-to-all-start.1) | async-done | bytes 131104 | tf_op jit(solution)/shard_map/all_to_all | solution.py:103
  214.1 3.5 %all-to-all-start.2 = ((f32[16,1,2048]{2,1,0:T(1,128)}), f32[16,1,2048]{2,1,0:T(1,128)S(1)}, u32[]{:S(2)}, u32[]{:S(2)}) async-start(f32[16,1,2048]{2,1,0:T(1,128)} %copy.14), calls=%async_computation.2 | async-start | bytes 262144 | tf_op jit(solution)/shard_map/all_to_all | solution.py:104
  217.9 0.7 reshape.260
  218.6 6.9 %all-to-all-done.2 = f32[16,1,2048]{2,1,0:T(1,128)S(1)} async-done(((f32[16,1,2048]{2,1,0:T(1,128)}), f32[16,1,2048]{2,1,0:T(1,128)S(1)}, u32[]{:S(2)}, u32[]{:S(2)}) %all-to-all-start.2) | async-done | bytes 131104 | tf_op jit(solution)/shard_map/all_to_all | solution.py:104
  225.8 0.7 reshape.261
  (125 shorter events, 5.7 us)
Async XLA Ops:
  0.7 56.8 %copy-start.2 = (s32[1,80]{1,0:T(1,128)S(1)}, s32[1,80]{1,0:T(1,128)}, u32[]{:S(2)}) copy-start(s32[1,80]{1,0:T(1,128)} %param.7) | copy-start | bytes 964
  78.4 3.1 %copy-start = (bf16[80,1,128]{1,0,2:T(8,128)(2,1)S(1)}, bf16[80,1,128]{1,0,2:T(8,128)(2,1)}, u32[]{:S(2)}) copy-start(bf16[80,1,128]{1,0,2:T(8,128)(2,1)} %get-tuple-element.244) | copy-start | bytes 61444
  78.4 6.0 %copy-start.1 = (f32[1,3,80]{2,0,1:T(1,128)S(1)}, f32[1,3,80]{2,0,1:T(1,128)}, u32[]{:S(2)}) copy-start(f32[1,3,80]{2,0,1:T(1,128)} %param.8) | copy-start | bytes 2884
  186.4 15.3 %all-to-all-start = ((f32[1,16,2048]{2,0,1:T(1,128)}), f32[1,16,2048]{2,0,1:T(1,128)S(1)}, u32[]{:S(2)}, u32[]{:S(2)}) async-start(f32[1,16,2048]{2,0,1:T(1,128)} %all_to_all.30), calls=%async_computation | async-start | bytes 262144 | tf_op jit(solution)/shard_map/all_to_all | solution.py:95
  202.7 11.4 %all-to-all-start.1 = ((f32[16,1,2048]{2,1,0:T(1,128)}), f32[16,1,2048]{2,1,0:T(1,128)S(1)}, u32[]{:S(2)}, u32[]{:S(2)}) async-start(f32[16,1,2048]{2,1,0:T(1,128)} %copy.13), calls=%async_computation.1 | async-start | bytes 262144 | tf_op jit(solution)/shard_map/all_to_all | solution.py:103
  214.1 11.4 %all-to-all-start.2 = ((f32[16,1,2048]{2,1,0:T(1,128)}), f32[16,1,2048]{2,1,0:T(1,128)S(1)}, u32[]{:S(2)}, u32[]{:S(2)}) async-start(f32[16,1,2048]{2,1,0:T(1,128)} %copy.14), calls=%async_computation.2 | async-start | bytes 262144 | tf_op jit(solution)/shard_map/all_to_all | solution.py:104
where the time goes:
time: 228 us; the launch traced here: 226 us
  other arithmetic  89.6 us (39%)
  local copies, waits for them, and re-layouts  88.7 us (39%)
  waiting for transfers between devices  21.8 us (10%)
  starting transfers between devices  14.4 us (6%)
  matrix products  9.69 us (4%)
    another operation x20, other arithmetic  87.8 us
    unnamed x8, local copies, waits for them, and re-layouts  56.8 us
    gather x1, local copies, waits for them, and re-layouts, spectrum_of(): lax.dynamic_slice_in_dim(one_row, offset, width, 1)  17.8 us
    dot_general x10, matrix products, block_product(): return jnp.dot(left, right, preferred_element_type=jnp.float32)  7.96 us
    all_to_all x1, waiting for transfers between devices, shards(): lax.all_to_all(flattened, 'sub', split_axis=1, concat_axis=0, tiled=True)  7.89 us
    all_to_all x1, starting transfers between devices, shards(): lax.all_to_all(flattened, 'sub', split_axis=1, concat_axis=0, tiled=True)  7.4 us
    all_to_all x1, waiting for transfers between devices, shards(): lax.all_to_all(frame_rows, 'sub', split_axis=0, concat_axis=1, tiled=True)  7 us
    all_to_all x1, waiting for transfers between devices, shards(): lax.all_to_all(cumulative_rows, 'sub', split_axis=0, concat_axis=1, tiled...  6.86 us
  transfers between devices with their start and end apart: 3, of which 3 were waited for; matrix products, arithmetic and copies ran while one was open for 1% of the time, Pallas kernels for 0%

commit v1 on v0

--- a/solution.py
+++ b/solution.py
@@ -100,7 +100,12 @@
     magnitude_factor = jnp.sqrt(jnp.arange(1, members + 1, dtype=jnp.int32).astype(jnp.float32))
     cumulative_rows = running / magnitude_factor[:, None]
     frames_back, cumulative_back = (
-        lax.all_to_all(frame_rows, "sub", split_axis=0, concat_axis=1, tiled=True),
+        jnp.concatenate(
+            lax.all_to_all(
+                jnp.stack(jnp.split(frame_rows, lax.axis_size("sub"), axis=0)), "sub", 0, 0
+            ),
+            axis=1,
+        ),
         lax.all_to_all(cumulative_rows, "sub", split_axis=0, concat_axis=1, tiled=True),
     )
     frames = frames_back.reshape(1, 2, rows, cols)

time: 228 us -> 237 us (1.039)
  local copies, waits for them, and re-layouts: 88.7 us -> 97.6 us
    unnamed x8 -> x23, local copies, waits for them, and re-layouts: 56.8 us -> 65.9 us
where the time goes in v1:
time: 237 us; the launch traced here: 235 us
  local copies, waits for them, and re-layouts  97.6 us (41%)
  other arithmetic  89.6 us (38%)
  waiting for transfers between devices  21.8 us (9%)
  starting transfers between devices  14.4 us (6%)
  matrix products  9.69 us (4%)
    another operation x20, other arithmetic  87.8 us
    unnamed x23, local copies, waits for them, and re-layouts  65.9 us
    gather x1, local copies, waits for them, and re-layouts, spectrum_of(): lax.dynamic_slice_in_dim(one_row, offset, width, 1)  17.8 us
    dot_general x10, matrix products, block_product(): return jnp.dot(left, right, preferred_element_type=jnp.float32)  7.96 us
    all_to_all x1, waiting for transfers between devices, shards(): lax.all_to_all(flattened, 'sub', split_axis=1, concat_axis=0, tiled=True)  7.89 us
    all_to_all x1, starting transfers between devices, shards(): lax.all_to_all(flattened, 'sub', split_axis=1, concat_axis=0, tiled=True)  7.4 us
    all_to_all x1, waiting for transfers between devices, shards(): lax.all_to_all(jnp.stack(jnp.split(frame_rows, lax.axis_size('sub'), axis...  7 us
    all_to_all x1, waiting for transfers between devices, shards(): lax.all_to_all(cumulative_rows, 'sub', split_axis=0, concat_axis=1, tiled...  6.86 us
  transfers between devices with their start and end apart: 3, of which 3 were waited for; matrix products, arithmetic and copies ran while one was open for 1% of the time, Pallas kernels for 0%

profile of v1, /device:TPU:0, one launch (start us, length us, event | category | flops | bytes accessed | tf_op | source)
XLA Modules:
  0.0 235.4 jit_solution(14946589354488242102)
XLA Ops:
  0.7 56.8 %copy.10 = bf16[1,80,2,4096]{2,1,3,0:T(8,128)(2,1)} copy(bf16[1,80,2,4096]{3,2,1,0:T(2,128)(2,1)} %param.6) | data formatting | bytes 2621440 | tf_op args[0]
  57.5 17.8 %gather_fusion = bf16[80,2,128]{1,0,2:T(8,128)(2,1)S(1)} fusion(bf16[80,2,4096]{1,0,2:T(8,128)(2,1)} %bitcast.1, s32[80]{0:T(128)S(1)} %fusion.56), kind=kCustom, calls=%fused_computation | custom fusion | bytes 82880 | tf_op jit(solution)/shard_map/vmap()/gather | solution.py:14
  75.3 3.2 %fusion.73 = (bf16[80,1,128]{1,0,2:T(8,128)(2,1)}, bf16[80,1,128]{1,0,2:T(8,128)(2,1)}) fusion(bf16[80,2,128]{1,0,2:T(8,128)(2,1)S(1)} %gather_fusion), kind=kLoop, calls=%fused_computation.133 | loop fusion | bytes 81920 | tf_op jit(solution)/shard_map/slice | solution.py:24
  78.4 3.1 %copy.11 = bf16[80,1,128]{2,0,1:T(8,128)(2,1)S(1)} copy(bf16[80,1,128]{1,0,2:T(8,128)(2,1)} %get-tuple-element.243) | data formatting | bytes 40960 | tf_op jit(solution)/shard_map/slice | solution.py:24
  81.5 1.6 copy.12
  85.5 100.0 %while.17 = (s32[]{:T(128)}, f32[32,1024]{1,0:T(8,128)S(1)}, f32[80,128]{1,0:T(8,128)S(1)}, f32[80]{0:T(128)S(1)}, f32[80,128]{1,0:T(8,128)S(1)}, /*index=5*/f32...) while((s32[]{:T(128)}, f32[32,1024]{1,0:T(8,128)S(1)}, ...), condition=%wide.region_1.2_spmd.clone.clone, body=%wide.region_0.1_spmd.clone.clone.sunk | while | flops 154242752 | bytes 6879337 | solution.py:92
  86.7 8.2 %fusion.81 = (bf16[1024,512]{1,0:T(8,128)(2,1)S(1)}, bf16[1024,512]{1,0:T(8,128)(2,1)S(1)}, bf16[1024,512]{1,0:T(8,128)(2,1)S(1)}) fusion(f32[512]{0:T(512)S(1)} %add_convert_fusion.4, f32[1024]{0:T(1024)S(1)} %bitcast_multiply_fusion.4), kind=kLoop, calls=%fused_computation.13.clone.1 | loop fusion | flops 2621440 | bytes 3151872 | tf_op jit(solution)/shard_map/convert.5
  94.9 0.8 fusion.83
  96.6 8.2 %fusion.81 = (bf16[1024,512]{1,0:T(8,128)(2,1)S(1)}, bf16[1024,512]{1,0:T(8,128)(2,1)S(1)}, bf16[1024,512]{1,0:T(8,128)(2,1)S(1)}) fusion(f32[512]{0:T(512)S(1)} %add_convert_fusion.4, f32[1024]{0:T(1024)S(1)} %bitcast_multiply_fusion.4), kind=kLoop, calls=%fused_computation.13.clone.1 | loop fusion | flops 2621440 | bytes 3151872 | tf_op jit(solution)/shard_map/convert.5
  104.9 0.8 fusion.83
  106.6 8.2 %fusion.81 = (bf16[1024,512]{1,0:T(8,128)(2,1)S(1)}, bf16[1024,512]{1,0:T(8,128)(2,1)S(1)}, bf16[1024,512]{1,0:T(8,128)(2,1)S(1)}) fusion(f32[512]{0:T(512)S(1)} %add_convert_fusion.4, f32[1024]{0:T(1024)S(1)} %bitcast_multiply_fusion.4), kind=kLoop, calls=%fused_computation.13.clone.1 | loop fusion | flops 2621440 | bytes 3151872 | tf_op jit(solution)/shard_map/convert.5
  114.9 0.8 fusion.83
  116.6 8.2 %fusion.81 = (bf16[1024,512]{1,0:T(8,128)(2,1)S(1)}, bf16[1024,512]{1,0:T(8,128)(2,1)S(1)}, bf16[1024,512]{1,0:T(8,128)(2,1)S(1)}) fusion(f32[512]{0:T(512)S(1)} %add_convert_fusion.4, f32[1024]{0:T(1024)S(1)} %bitcast_multiply_fusion.4), kind=kLoop, calls=%fused_computation.13.clone.1 | loop fusion | flops 2621440 | bytes 3151872 | tf_op jit(solution)/shard_map/convert.5
  124.8 0.8 fusion.83
  126.6 8.2 %fusion.81 = (bf16[1024,512]{1,0:T(8,128)(2,1)S(1)}, bf16[1024,512]{1,0:T(8,128)(2,1)S(1)}, bf16[1024,512]{1,0:T(8,128)(2,1)S(1)}) fusion(f32[512]{0:T(512)S(1)} %add_convert_fusion.4, f32[1024]{0:T(1024)S(1)} %bitcast_multiply_fusion.4), kind=kLoop, calls=%fused_computation.13.clone.1 | loop fusion | flops 2621440 | bytes 3151872 | tf_op jit(solution)/shard_map/convert.5
  134.8 0.8 fusion.83
  136.6 8.2 %fusion.81 = (bf16[1024,512]{1,0:T(8,128)(2,1)S(1)}, bf16[1024,512]{1,0:T(8,128)(2,1)S(1)}, bf16[1024,512]{1,0:T(8,128)(2,1)S(1)}) fusion(f32[512]{0:T(512)S(1)} %add_convert_fusion.4, f32[1024]{0:T(1024)S(1)} %bitcast_multiply_fusion.4), kind=kLoop, calls=%fused_computation.13.clone.1 | loop fusion | flops 2621440 | bytes 3151872 | tf_op jit(solution)/shard_map/convert.5
  144.8 0.8 fusion.83
  146.5 8.2 %fusion.81 = (bf16[1024,512]{1,0:T(8,128)(2,1)S(1)}, bf16[1024,512]{1,0:T(8,128)(2,1)S(1)}, bf16[1024,512]{1,0:T(8,128)(2,1)S(1)}) fusion(f32[512]{0:T(512)S(1)} %add_convert_fusion.4, f32[1024]{0:T(1024)S(1)} %bitcast_multiply_fusion.4), kind=kLoop, calls=%fused_computation.13.clone.1 | loop fusion | flops 2621440 | bytes 3151872 | tf_op jit(solution)/shard_map/convert.5
  154.8 0.8 fusion.83
  156.5 8.2 %fusion.81 = (bf16[1024,512]{1,0:T(8,128)(2,1)S(1)}, bf16[1024,512]{1,0:T(8,128)(2,1)S(1)}, bf16[1024,512]{1,0:T(8,128)(2,1)S(1)}) fusion(f32[512]{0:T(512)S(1)} %add_convert_fusion.4, f32[1024]{0:T(1024)S(1)} %bitcast_multiply_fusion.4), kind=kLoop, calls=%fused_computation.13.clone.1 | loop fusion | flops 2621440 | bytes 3151872 | tf_op jit(solution)/shard_map/convert.5
  164.8 0.8 fusion.83
  166.5 8.2 %fusion.81 = (bf16[1024,512]{1,0:T(8,128)(2,1)S(1)}, bf16[1024,512]{1,0:T(8,128)(2,1)S(1)}, bf16[1024,512]{1,0:T(8,128)(2,1)S(1)}) fusion(f32[512]{0:T(512)S(1)} %add_convert_fusion.4, f32[1024]{0:T(1024)S(1)} %bitcast_multiply_fusion.4), kind=kLoop, calls=%fused_computation.13.clone.1 | loop fusion | flops 2621440 | bytes 3151872 | tf_op jit(solution)/shard_map/convert.5
  174.7 0.8 fusion.83
  176.5 8.2 %fusion.81 = (bf16[1024,512]{1,0:T(8,128)(2,1)S(1)}, bf16[1024,512]{1,0:T(8,128)(2,1)S(1)}, bf16[1024,512]{1,0:T(8,128)(2,1)S(1)}) fusion(f32[512]{0:T(512)S(1)} %add_convert_fusion.4, f32[1024]{0:T(1024)S(1)} %bitcast_multiply_fusion.4), kind=kLoop, calls=%fused_computation.13.clone.1 | loop fusion | flops 2621440 | bytes 3151872 | tf_op jit(solution)/shard_map/convert.5
  184.7 0.8 fusion.83
  185.6 0.8 all_to_all.23
  186.4 7.4 %all-to-all-start = ((f32[1,16,2048]{2,0,1:T(1,128)}), f32[1,16,2048]{2,0,1:T(1,128)S(1)}, u32[]{:S(2)}, u32[]{:S(2)}) async-start(f32[1,16,2048]{2,0,1:T(1,128)} %all_to_all.23), calls=%async_computation | async-start | bytes 262144 | tf_op jit(solution)/shard_map/all_to_all | solution.py:95
  193.8 7.9 %all-to-all-done = f32[1,16,2048]{2,0,1:T(1,128)S(1)} async-done(((f32[1,16,2048]{2,0,1:T(1,128)}), f32[1,16,2048]{2,0,1:T(1,128)S(1)}, u32[]{:S(2)}, u32[]{:S(2)}) %all-to-all-start) | async-done | bytes 131104 | tf_op jit(solution)/shard_map/all_to_all | solution.py:95
  202.5 0.6 constant_dynamic-update-slice_fusion.14
  203.1 0.6 constant_dynamic-update-slice_fusion.13
  203.7 0.6 constant_dynamic-update-slice_fusion.12
  204.3 0.6 constant_dynamic-update-slice_fusion.11
  204.9 0.6 constant_dynamic-update-slice_fusion.10
  205.5 0.6 constant_dynamic-update-slice_fusion.9
  206.1 0.6 constant_dynamic-update-slice_fusion.8
  207.3 0.6 constant_dynamic-update-slice_fusion.6
  207.9 0.6 constant_dynamic-update-slice_fusion.5
  208.5 0.6 constant_dynamic-update-slice_fusion.4
  210.4 0.6 constant_dynamic-update-slice_fusion.1
  211.0 0.6 constant_dynamic-update-slice_fusion
  211.6 3.5 %all-to-all-start.1 = ((f32[16,1,2048]{2,1,0:T(1,128)}), f32[16,1,2048]{2,1,0:T(1,128)S(1)}, u32[]{:S(2)}, u32[]{:S(2)}) async-start(f32[16,1,2048]{2,1,0:T(1,128)} %constant_dynamic-update-slice_fusion), calls=%async_computation.1 | async-start | bytes 262144 | tf_op jit(solution)/shard_map/all_to_all | solution.py:104
  215.2 0.8 copy.13
  216.0 7.0 %all-to-all-done.1 = f32[16,1,2048]{2,1,0:T(1,128)S(1)} async-done(((f32[16,1,2048]{2,1,0:T(1,128)}), f32[16,1,2048]{2,1,0:T(1,128)S(1)}, u32[]{:S(2)}, u32[]{:S(2)}) %all-to-all-start.1) | async-done | bytes 131104 | tf_op jit(solution)/shard_map/all_to_all | solution.py:104
  223.0 3.5 %all-to-all-start.2 = ((f32[16,1,2048]{2,1,0:T(1,128)}), f32[16,1,2048]{2,1,0:T(1,128)S(1)}, u32[]{:S(2)}, u32[]{:S(2)}) async-start(f32[16,1,2048]{2,1,0:T(1,128)} %copy.13), calls=%async_computation.2 | async-start | bytes 262144 | tf_op jit(solution)/shard_map/all_to_all | solution.py:109
  226.8 0.7 reshape_reshape.3
  227.5 6.9 %all-to-all-done.2 = f32[16,1,2048]{2,1,0:T(1,128)S(1)} async-done(((f32[16,1,2048]{2,1,0:T(1,128)}), f32[16,1,2048]{2,1,0:T(1,128)S(1)}, u32[]{:S(2)}, u32[]{:S(2)}) %all-to-all-start.2) | async-done | bytes 131104 | tf_op jit(solution)/shard_map/all_to_all | solution.py:109
  234.7 0.7 reshape.250
  (140 shorter events, 14.1 us)
Async XLA Ops:
  0.7 56.8 %copy-start.2 = (s32[1,80]{1,0:T(1,128)S(1)}, s32[1,80]{1,0:T(1,128)}, u32[]{:S(2)}) copy-start(s32[1,80]{1,0:T(1,128)} %param.7) | copy-start | bytes 964
  78.4 3.1 %copy-start = (bf16[80,1,128]{1,0,2:T(8,128)(2,1)S(1)}, bf16[80,1,128]{1,0,2:T(8,128)(2,1)}, u32[]{:S(2)}) copy-start(bf16[80,1,128]{1,0,2:T(8,128)(2,1)} %get-tuple-element.244) | copy-start | bytes 61444
  78.4 6.0 %copy-start.1 = (f32[1,3,80]{2,0,1:T(1,128)S(1)}, f32[1,3,80]{2,0,1:T(1,128)}, u32[]{:S(2)}) copy-start(f32[1,3,80]{2,0,1:T(1,128)} %param.8) | copy-start | bytes 2884
  186.4 15.3 %all-to-all-start = ((f32[1,16,2048]{2,0,1:T(1,128)}), f32[1,16,2048]{2,0,1:T(1,128)S(1)}, u32[]{:S(2)}, u32[]{:S(2)}) async-start(f32[1,16,2048]{2,0,1:T(1,128)} %all_to_all.23), calls=%async_computation | async-start | bytes 262144 | tf_op jit(solution)/shard_map/all_to_all | solution.py:95
  211.6 11.4 %all-to-all-start.1 = ((f32[16,1,2048]{2,1,0:T(1,128)}), f32[16,1,2048]{2,1,0:T(1,128)S(1)}, u32[]{:S(2)}, u32[]{:S(2)}) async-start(f32[16,1,2048]{2,1,0:T(1,128)} %constant_dynamic-update-slice_fusion), calls=%async_computation.1 | async-start | bytes 262144 | tf_op jit(solution)/shard_map/all_to_all | solution.py:104
  223.0 11.4 %all-to-all-start.2 = ((f32[16,1,2048]{2,1,0:T(1,128)}), f32[16,1,2048]{2,1,0:T(1,128)S(1)}, u32[]{:S(2)}, u32[]{:S(2)}) async-start(f32[16,1,2048]{2,1,0:T(1,128)} %copy.13), calls=%async_computation.2 | async-start | bytes 262144 | tf_op jit(solution)/shard_map/all_to_all | solution.py:109
